TPU v7x, 32 devices: a whole 2x2x4 slice. The times are simulated.
32 devices in a mesh: row: 4 (over y, x), col: 8 (over z, core).
Axes of the slice: x: 2, y: 2, z: 4, core: 2. Of those that a mesh axis runs over, the one named last changes fastest.
Arguments:
- queries: bfloat16 [32, 128, 512], P('row', 'col'), may hold values from -6 to 6
- keys: bfloat16 [32, 128, 512], P('row', 'col'), may hold values from -6 to 6
- values: bfloat16 [32, 128, 512], P('row', 'col'), may hold values from -6 to 6
- grad_out: bfloat16 [32, 128, 512], P('row', 'col'), may hold values from -6 to 6
- rel_bias: float32 [8, 17, 17], replicated, may hold values from -4 to 4
- occupied: int32 [4, 8], replicated, may hold values 0 or 1
Outputs:
- grad_queries: bfloat16 [32, 128, 512], P('row', 'col')
- grad_keys: bfloat16 [32, 128, 512], P('row', 'col')
- grad_values: bfloat16 [32, 128, 512], P('row', 'col')
- grad_bias: float32 [8, 17, 17], replicated
All inputs are finite; a program needn't handle non-finite values.
Results may differ from a plain program's by a relative error of at most 0.015.
Values may be sent and summed in bfloat16 or wider, within the bound.
A program may use at most 64 MiB of HBM per device.

v0:
```python
import jax
import jax.numpy as jnp
from jax import lax
from jax.sharding import PartitionSpec as P


def from_behind(value, axis, steps):
    count = lax.axis_size(axis)
    first, last = (max(0, -steps), min(count, count - steps))
    return lax.ppermute(value, axis, [(source, source + steps) for source in range(first, last)])


def with_halo(block, sides, width):
    for axis, dim in sides:
        count = lax.axis_size(axis)
        forward = [(i, i + 1) for i in range(count - 1)]
        backward = [(target, source) for source, target in forward]
        low = lax.ppermute(
            lax.slice_in_dim(block, block.shape[dim] - width, None, axis=dim), axis, forward
        )
        high = lax.ppermute(lax.slice_in_dim(block, 0, width, axis=dim), axis, backward)
        block = jnp.concatenate([low, block, high], axis=dim)
    return block


def offset_table(first_count, second_count, direction, window_span):
    table_shape = (first_count, second_count, window_span)
    first_index = lax.broadcasted_iota(jnp.int32, table_shape, 0)
    second_index = lax.broadcasted_iota(jnp.int32, table_shape, 1)
    slot_index = lax.broadcasted_iota(jnp.int32, table_shape, 2)
    return (direction * (second_index - first_index) == slot_index).astype(jnp.float32)


def expand_part(table_rows, table_cols, bias_part):
    partial_bias = jnp.einsum(
        "cqe,de->cqd", table_cols, bias_part, preferred_element_type=jnp.float32
    ).astype(jnp.bfloat16)
    return jnp.einsum("rpd,cqd->rcpq", table_rows, partial_bias, preferred_element_type=jnp.float32)


def expand_bias(table_rows, table_cols, bias_head):
    rows_low = table_rows.astype(jnp.bfloat16)
    cols_low = table_cols.astype(jnp.bfloat16)
    bias_high = bias_head.astype(jnp.bfloat16)
    bias_rest = (bias_head - bias_high.astype(jnp.float32)).astype(jnp.bfloat16)
    full_bias = expand_part(rows_low, cols_low, bias_high) + expand_part(
        rows_low, cols_low, bias_rest
    )
    return full_bias.reshape(
        full_bias.shape[0] * full_bias.shape[1], full_bias.shape[2] * full_bias.shape[3]
    )


def bias_gradient(grad_grid, window_span):
    tile_rows, tile_cols, padded_rows, padded_cols = grad_grid.shape
    by_rows = jnp.transpose(grad_grid, (0, 2, 1, 3)).reshape(
        tile_rows * padded_rows, tile_cols, padded_cols
    )
    by_rows = jnp.pad(by_rows, ((0, tile_rows), (0, 0), (0, 0)))
    by_rows = by_rows.reshape(tile_rows, padded_rows + 1, tile_cols, padded_cols)[:, :window_span]
    row_summed = jnp.sum(by_rows, axis=0).reshape(window_span, tile_cols * padded_cols)
    row_summed = jnp.pad(row_summed, ((0, 0), (0, tile_cols)))
    skewed = row_summed.reshape(window_span, tile_cols, padded_cols + 1)[:, :, :window_span]
    return jnp.sum(skewed, axis=1)


def allowed_pairs(table_rows, table_cols, cell_filled):
    row_inside = jnp.sum(table_rows, axis=2)
    col_inside = jnp.sum(table_cols, axis=2)
    joint = (
        row_inside[:, None, :, None] * col_inside[None, :, None, :] * cell_filled[None, None, :, :]
    )
    return joint.reshape(joint.shape[0] * joint.shape[1], joint.shape[2] * joint.shape[3]) > 0.5


def pick_tiles(extent, radius):
    cell_shape = (extent + 2 * radius, 3)
    position = lax.broadcasted_iota(jnp.int32, cell_shape, 0)
    tile_index = lax.broadcasted_iota(jnp.int32, cell_shape, 1)
    tile_of_cell = (position >= radius).astype(jnp.int32) + (position >= radius + extent).astype(
        jnp.int32
    )
    return (tile_of_cell == tile_index).astype(jnp.float32)


def neighbour_cells(nearby, tile_rows, tile_cols, radius):
    pick_rows = pick_tiles(tile_rows, radius)
    pick_cols = pick_tiles(tile_cols, radius)
    inner_rows = jnp.dot(pick_rows, nearby, precision=lax.Precision.HIGHEST)
    return jnp.dot(inner_rows, pick_cols.T, precision=lax.Precision.HIGHEST)


def head_slice(matrix, head_index, head_width):
    return lax.dynamic_slice_in_dim(matrix, head_index * head_width, head_width, 1)


def fold_columns(partials, radius):
    interior = partials.shape[2] - 2 * radius
    from_after = from_behind(partials[:, :, :radius].astype(jnp.bfloat16), "col", -1).astype(
        jnp.float32
    )
    from_before = from_behind(
        partials[:, :, radius + interior :].astype(jnp.bfloat16), "col", 1
    ).astype(jnp.float32)
    middle = partials[:, :, radius : radius + interior]
    middle = middle.at[:, :, :radius].add(from_before)
    return middle.at[:, :, interior - radius :].add(from_after)


def fold_rows(partials, radius):
    interior = partials.shape[1] - 2 * radius
    from_after = from_behind(partials[:, :radius].astype(jnp.bfloat16), "row", -1).astype(
        jnp.float32
    )
    from_before = from_behind(
        partials[:, radius + interior :].astype(jnp.bfloat16), "row", 1
    ).astype(jnp.float32)
    middle = partials[:, radius : radius + interior]
    middle = middle.at[:, :radius].add(from_before)
    return middle.at[:, interior - radius :].add(from_after)


def transposed_dot(left_matrix, right_matrix):
    return lax.dot_general(
        left_matrix, right_matrix, (((0,), (0,)), ((), ())), preferred_element_type=jnp.float32
    )


def rows_dot(left_matrix, right_matrix):
    return lax.dot_general(
        left_matrix, right_matrix, (((1,), (1,)), ((), ())), preferred_element_type=jnp.float32
    )


def shards(queries, keys, values, grad_out, rel_bias, occupied):
    tile_rows, tile_cols, model_width = queries.shape
    head_count = rel_bias.shape[0]
    window_span = rel_bias.shape[1]
    radius = (window_span - 1) // 2
    head_width = model_width // head_count
    score_scale = head_width ** (-0.5)
    padded_rows = tile_rows + 2 * radius
    padded_cols = tile_cols + 2 * radius
    query_count = tile_rows * tile_cols
    padded_count = padded_rows * padded_cols
    row_index = lax.axis_index("row")
    col_index = lax.axis_index("col")
    nearby = lax.dynamic_slice(jnp.pad(occupied, 1), (row_index, col_index), (3, 3)).astype(
        jnp.float32
    )
    own_tile = nearby[1, 1]
    cell_filled = neighbour_cells(nearby, tile_rows, tile_cols, radius)
    key_value_halo = with_halo(jnp.stack((keys, values)), (("row", 1), ("col", 2)), radius)
    key_matrix = key_value_halo[0].reshape(padded_count, model_width)
    value_matrix = key_value_halo[1].reshape(padded_count, model_width)
    query_matrix = queries.reshape(query_count, model_width)
    grad_matrix = grad_out.reshape(query_count, model_width)
    forward_rows = offset_table(tile_rows, padded_rows, 1, window_span)
    forward_cols = offset_table(tile_cols, padded_cols, 1, window_span)
    forward_allowed = allowed_pairs(forward_rows, forward_cols, cell_filled)
    partial_shape = (padded_count, model_width)

    def query_pass(head_index, carried):
        grad_query, grad_key, grad_value, log_total, delta_all, grad_bias = carried
        query_head = head_slice(query_matrix, head_index, head_width)
        key_head = head_slice(key_matrix, head_index, head_width)
        value_head = head_slice(value_matrix, head_index, head_width)
        grad_head = head_slice(grad_matrix, head_index, head_width)
        bias_head = lax.dynamic_index_in_dim(rel_bias, head_index, 0, keepdims=False)
        scores = rows_dot(query_head, key_head) * score_scale + expand_bias(
            forward_rows, forward_cols, bias_head
        )
        scores = jnp.where(forward_allowed, scores, -jnp.inf)
        row_max = jnp.max(scores, axis=1, keepdims=True)
        exponent = jnp.exp(scores - row_max)
        row_total = jnp.sum(exponent, axis=1, keepdims=True)
        weights = exponent / row_total
        grad_weights = rows_dot(grad_head, value_head)
        row_delta = jnp.sum(weights * grad_weights, axis=1, keepdims=True)
        grad_scores = weights * (grad_weights - row_delta)
        weights_low = weights.astype(jnp.bfloat16)
        grad_scores_low = grad_scores.astype(jnp.bfloat16)
        query_term = (
            jnp.dot(grad_scores_low, key_head, preferred_element_type=jnp.float32) * score_scale
        )
        grad_query = lax.dynamic_update_slice_in_dim(
            grad_query, query_term, head_index * head_width, 1
        )
        bias_term = bias_gradient(
            grad_scores.reshape(tile_rows, tile_cols, padded_rows, padded_cols), window_span
        )
        grad_bias = lax.dynamic_update_index_in_dim(grad_bias, bias_term, head_index, 0)
        log_total = lax.dynamic_update_slice_in_dim(
            log_total, row_max + jnp.log(row_total), head_index, 1
        )
        delta_all = lax.dynamic_update_slice_in_dim(delta_all, row_delta, head_index, 1)
        key_term = transposed_dot(grad_scores_low, query_head) * score_scale
        value_term = transposed_dot(weights_low, grad_head)
        grad_key = lax.dynamic_update_slice_in_dim(grad_key, key_term, head_index * head_width, 1)
        grad_value = lax.dynamic_update_slice_in_dim(
            grad_value, value_term, head_index * head_width, 1
        )
        return (grad_query, grad_key, grad_value, log_total, delta_all, grad_bias)

    initial = (
        jnp.zeros((query_count, model_width), jnp.float32),
        jnp.zeros(partial_shape, jnp.float32),
        jnp.zeros(partial_shape, jnp.float32),
        jnp.zeros((query_count, head_count), jnp.float32),
        jnp.zeros((query_count, head_count), jnp.float32),
        jnp.zeros((head_count, window_span, window_span), jnp.float32),
    )

    def run_queries():
        return lax.fori_loop(0, head_count, query_pass, initial)

    def skip_queries():
        return initial

    grad_query, grad_key, grad_value, log_total, delta_all, grad_bias = lax.cond(
        own_tile > 0.5, run_queries, skip_queries
    )
    bias_summed = lax.psum(grad_bias, ("row", "col"))
    query_grads = grad_query.astype(jnp.bfloat16).reshape(tile_rows, tile_cols, model_width)
    partials = jnp.stack((grad_key, grad_value)).reshape(2, padded_rows, padded_cols, model_width)
    owned_grads = fold_rows(fold_columns(partials, radius), radius)
    return (
        query_grads,
        owned_grads[0].astype(jnp.bfloat16),
        owned_grads[1].astype(jnp.bfloat16),
        bias_summed,
    )


def solution(mesh):
    placed = (
        P("row", "col", None),
        P("row", "col", None),
        P("row", "col", None),
        P("row", "col", None),
        P(),
        P(),
    )
    return jax.shard_map(
        shards,
        mesh=mesh,
        in_specs=placed,
        out_specs=(P("row", "col", None), P("row", "col", None), P("row", "col", None), P()),
        check_vma=False,
    )
```

profile of v0, /device:TPU:0, one launch (start us, length us, event | category | flops | bytes accessed | tf_op | source)
XLA Modules:
  0.0 246.2 jit_solution(10566615659084771039)
XLA Ops:
  0.6 1.0 pad_maximum_fusion.2
  1.6 1.3 collective-permute-start.1
  2.9 5.5 %collective-permute-start = (bf16[2,8,16,512]{3,2,1,0:T(8,128)(2,1)S(1)}, bf16[2,8,16,512]{3,2,1,0:T(8,128)(2,1)S(1)}, u32[]{:S(2)}, u32[]{:S(2)}) collective-permute-start(bf16[2,8,16,512]{3,2,1,0:T(8,128)(2,1)S(1)} %pad_maximum_fusion.2), channel_id=1, source_target_pairs={{0,8},{8,16},{16,24},{1,9},{9,17},{17,25},{2,10},{10,18},{18,26},{... | collective-permute-start | bytes 786440 | tf_op jit(solution)/shard_map/ppermute | solution.py:18
  8.5 0.8 fusion.52
  9.3 0.2 fusion.49
  9.4 0.0 copy-start.3
  9.4 0.0 copy-start.4
  9.4 4.2 %collective-permute-done.1 = bf16[2,8,16,512]{3,2,1,0:T(8,128)(2,1)S(1)} collective-permute-done((bf16[2,8,16,512]{3,2,1,0:T(8,128)(2,1)S(1)}, bf16[2,8,16,512]{3,2,1,0:T(8,128)(2,1)S(1)}, u32[]{:S(2)}, u32[]{:S(2)}) %collective-permute-start.1) | collective-permute-done | bytes 262176 | tf_op jit(solution)/shard_map/ppermute | solution.py:21
  13.7 0.3 collective-permute-done
  14.0 1.1 pad_maximum_fusion.1
  15.0 0.1 fusion.59
  15.1 1.3 collective-permute-start.2
  16.4 1.3 collective-permute-start.3
  17.7 0.6 slice.176
  19.0 0.2 fusion.48
  19.2 0.0 collective-permute-done.2
  19.2 2.8 %collective-permute-done.3 = bf16[2,24,8,512]{3,2,1,0:T(8,128)(2,1)S(1)} collective-permute-done((bf16[2,24,8,512]{3,2,1,0:T(8,128)(2,1)S(1)}, bf16[2,24,8,512]{3,2,1,0:T(8,128)(2,1)S(1)}, u32[]{:S(2)}, u32[]{:S(2)}) %collective-permute-start.3) | collective-permute-done | bytes 393248 | tf_op jit(solution)/shard_map/ppermute | solution.py:21
  22.1 0.0 copy-done.3
  22.1 0.0 copy-done.4
  22.1 0.2 pad_maximum_fusion
  22.3 2.7 %conditional.1 = (f32[8,17,17]{2,1,0:T(8,128)S(1)}, bf16[8,16,512]{2,1,0:T(8,128)(2,1)S(1)}, f32[1,24,32,512]{3,2,1,0:T(8,128)}, f32[1,24,32,512]{3,2,1,0:T(8,128)}) conditional(s32[]{:T(128)} %bitcast.7, () %tuple.69, (bf16[8,16,512]{2,1,0:T(8,128)(2,1)}, bf16[2,24,32,512]{3,2,1,0:T(8,128)(2,1)S(1)}, bf16[8,16,512]{2,1,0:T(8,128)(2,1)}, ...), branch_computations={%region_0.1_spmd, %region_1.11_spmd} | conditional | flops 72604152 | bytes 37085184 | solution.py:220
  22.3 1.4 stack.5.clone
  23.7 1.3 stack.5
  25.0 0.0 copy-start.6
  25.0 1.6 constant_dynamic-update-slice_fusion.1
  26.6 0.0 copy-done.6
  26.6 1.5 constant_dynamic-update-slice_fusion
  28.1 0.2 convert.13
  28.4 0.1 fusion.57
  28.5 154.9 %collective-permute-start.4 = (bf16[2,24,8,512]{3,2,1,0:T(8,128)(2,1)S(1)}, bf16[2,24,8,512]{3,2,1,0:T(8,128)(2,1)S(1)}, u32[]{:S(2)}, u32[]{:S(2)}) collective-permute-start(bf16[2,24,8,512]{3,2,1,0:T(8,128)(2,1)S(1)} %get-tuple-element.623), channel_id=1, source_target_pairs={{0,1},{1,2},{2,3},{3,4},{4,5},{5,6},{6,7},{8,9},{9,10},{10,11},{11... | collective-permute-start | bytes 1179656 | tf_op jit(solution)/shard_map/ppermute | solution.py:10
  183.4 1.3 collective-permute-start.5
  184.7 0.1 slice.195
  184.8 0.0 collective-permute-done.4
  184.8 0.1 fusion.43
  184.9 2.0 collective-permute-done.5
  187.0 0.2 fusion.42
  187.2 0.1 convert.14
  187.4 5.9 %collective-permute-start.6 = (bf16[2,8,16,512]{3,2,1,0:T(8,128)(2,1)S(1)}, bf16[2,8,16,512]{3,2,1,0:T(8,128)(2,1)S(1)}, u32[]{:S(2)}, u32[]{:S(2)}) collective-permute-start(bf16[2,8,16,512]{3,2,1,0:T(8,128)(2,1)S(1)} %get-tuple-element.624), channel_id=1, source_target_pairs={{0,8},{8,16},{16,24},{1,9},{9,17},{17,25},{2,10},{10,18},{18,26},{... | collective-permute-start | bytes 786440 | tf_op jit(solution)/shard_map/ppermute | solution.py:10
  193.3 1.3 collective-permute-start.7
  194.6 50.8 %psum.7 = f32[8,17,17]{2,0,1:T(8,128)} all-reduce(f32[8,17,17]{2,0,1:T(8,128)S(1)} %copy.61), channel_id=1, replica_groups=mesh['row'=4,'col'=8] {'row','col'}, use_global_device_ids=true, to_apply=%region_11.12 | all-reduce | flops 2312 | bytes 18496 | tf_op jit(solution)/shard_map/psum | solution.py:223
  245.4 0.0 collective-permute-done.6
  245.4 0.0 collective-permute-done.7
  245.4 0.1 fusion.45
  245.5 0.7 slice_bitcast_fusion
  (8 shorter events, 0.1 us)
Async XLA Ops:
  1.6 12.0 %collective-permute-start.1 = (bf16[2,8,16,512]{3,2,1,0:T(8,128)(2,1)S(1)}, bf16[2,8,16,512]{3,2,1,0:T(8,128)(2,1)S(1)}, u32[]{:S(2)}, u32[]{:S(2)}) collective-permute-start(bf16[2,8,16,512]{3,2,1,0:T(8,128)(2,1)S(1)} %pad_maximum_fusion.2), channel_id=1, source_target_pairs={{8,0},{16,8},{24,16},{9,1},{17,9},{25,17},{10,2},{18,10},{26,18},{... | collective-permute-start | bytes 786440 | tf_op jit(solution)/shard_map/ppermute | solution.py:21
  2.9 11.1 %collective-permute-start = (bf16[2,8,16,512]{3,2,1,0:T(8,128)(2,1)S(1)}, bf16[2,8,16,512]{3,2,1,0:T(8,128)(2,1)S(1)}, u32[]{:S(2)}, u32[]{:S(2)}) collective-permute-start(bf16[2,8,16,512]{3,2,1,0:T(8,128)(2,1)S(1)} %pad_maximum_fusion.2), channel_id=1, source_target_pairs={{0,8},{8,16},{16,24},{1,9},{9,17},{17,25},{2,10},{10,18},{18,26},{... | collective-permute-start | bytes 786440 | tf_op jit(solution)/shard_map/ppermute | solution.py:18
  9.4 12.6 %copy-start.3 = (bf16[8,16,512]{2,1,0:T(8,128)(2,1)S(1)}, bf16[8,16,512]{2,1,0:T(8,128)(2,1)}, u32[]{:S(2)}) copy-start(bf16[8,16,512]{2,1,0:T(8,128)(2,1)} %param.24) | copy-start | bytes 393220
  9.4 12.6 %copy-start.4 = (bf16[8,16,512]{2,1,0:T(8,128)(2,1)S(1)}, bf16[8,16,512]{2,1,0:T(8,128)(2,1)}, u32[]{:S(2)}) copy-start(bf16[8,16,512]{2,1,0:T(8,128)(2,1)} %param.23) | copy-start | bytes 393220
  15.1 4.1 %collective-permute-start.2 = (bf16[2,24,8,512]{3,2,1,0:T(8,128)(2,1)S(1)}, bf16[2,24,8,512]{3,2,1,0:T(8,128)(2,1)S(1)}, u32[]{:S(2)}, u32[]{:S(2)}) collective-permute-start(bf16[2,24,8,512]{3,2,1,0:T(8,128)(2,1)S(1)} %get-tuple-element.626), channel_id=1, source_target_pairs={{0,1},{1,2},{2,3},{3,4},{4,5},{5,6},{6,7},{8,9},{9,10},{10,11},{11... | collective-permute-start | bytes 1179656 | tf_op jit(solution)/shard_map/ppermute | solution.py:18
  16.4 5.6 %collective-permute-start.3 = (bf16[2,24,8,512]{3,2,1,0:T(8,128)(2,1)S(1)}, bf16[2,24,8,512]{3,2,1,0:T(8,128)(2,1)S(1)}, u32[]{:S(2)}, u32[]{:S(2)}) collective-permute-start(bf16[2,24,8,512]{3,2,1,0:T(8,128)(2,1)S(1)} %get-tuple-element.627), channel_id=1, source_target_pairs={{1,0},{2,1},{3,2},{4,3},{5,4},{6,5},{7,6},{9,8},{10,9},{11,10},{12... | collective-permute-start | bytes 1179656 | tf_op jit(solution)/shard_map/ppermute | solution.py:21
  25.0 1.6 copy-start.6
  28.5 156.4 %collective-permute-start.4 = (bf16[2,24,8,512]{3,2,1,0:T(8,128)(2,1)S(1)}, bf16[2,24,8,512]{3,2,1,0:T(8,128)(2,1)S(1)}, u32[]{:S(2)}, u32[]{:S(2)}) collective-permute-start(bf16[2,24,8,512]{3,2,1,0:T(8,128)(2,1)S(1)} %get-tuple-element.623), channel_id=1, source_target_pairs={{0,1},{1,2},{2,3},{3,4},{4,5},{5,6},{6,7},{8,9},{9,10},{10,11},{11... | collective-permute-start | bytes 1179656 | tf_op jit(solution)/shard_map/ppermute | solution.py:10
  183.4 3.6 %collective-permute-start.5 = (bf16[2,24,8,512]{3,2,1,0:T(8,128)(2,1)S(1)}, bf16[2,24,8,512]{3,2,1,0:T(8,128)(2,1)S(1)}, u32[]{:S(2)}, u32[]{:S(2)}) collective-permute-start(bf16[2,24,8,512]{3,2,1,0:T(8,128)(2,1)S(1)} %get-tuple-element.622), channel_id=1, source_target_pairs={{1,0},{2,1},{3,2},{4,3},{5,4},{6,5},{7,6},{9,8},{10,9},{11,10},{12... | collective-permute-start | bytes 1179656 | tf_op jit(solution)/shard_map/ppermute | solution.py:10
  187.4 58.0 %collective-permute-start.6 = (bf16[2,8,16,512]{3,2,1,0:T(8,128)(2,1)S(1)}, bf16[2,8,16,512]{3,2,1,0:T(8,128)(2,1)S(1)}, u32[]{:S(2)}, u32[]{:S(2)}) collective-permute-start(bf16[2,8,16,512]{3,2,1,0:T(8,128)(2,1)S(1)} %get-tuple-element.624), channel_id=1, source_target_pairs={{0,8},{8,16},{16,24},{1,9},{9,17},{17,25},{2,10},{10,18},{18,26},{... | collective-permute-start | bytes 786440 | tf_op jit(solution)/shard_map/ppermute | solution.py:10
  193.3 52.1 %collective-permute-start.7 = (bf16[2,8,16,512]{3,2,1,0:T(8,128)(2,1)S(1)}, bf16[2,8,16,512]{3,2,1,0:T(8,128)(2,1)S(1)}, u32[]{:S(2)}, u32[]{:S(2)}) collective-permute-start(bf16[2,8,16,512]{3,2,1,0:T(8,128)(2,1)S(1)} %get-tuple-element.625), channel_id=1, source_target_pairs={{8,0},{16,8},{24,16},{9,1},{17,9},{25,17},{10,2},{18,10},{26,18},{... | collective-permute-start | bytes 786440 | tf_op jit(solution)/shard_map/ppermute | solution.py:10
where the time goes:
time: 249 us; the launch traced here: 246 us
  starting transfers between devices  173 us (69%)
  blocking collectives  50.8 us (20%)
  waiting for transfers between devices  9.44 us (4%)
  local copies, waits for them, and re-layouts  7.44 us (3%)
  other arithmetic  3.82 us (2%)
    ppermute x4, starting transfers between devices, from_behind(): lax.ppermute(value, axis, [(source, source + steps) for source in range(f...  163 us
    psum x1, blocking collectives, shards(): bias_summed = lax.psum(grad_bias, ('row', 'col'))  50.8 us
    ppermute x2, waiting for transfers between devices, with_halo(): lax.ppermute(lax.slice_in_dim(block, 0, width, axis=dim), axis, backward)  7.05 us
    ppermute x2, starting transfers between devices, with_halo(): lax.ppermute(lax.slice_in_dim(block, block.shape[dim] - width, None, axis...  6.83 us
  transfers between devices with their start and end apart: 8, of which 4 were waited for; matrix products, arithmetic and copies ran while one was open for 1% of the time, Pallas kernels for 0%

commit v1 on v0

--- a/solution.py
+++ b/solution.py
@@ -220,7 +220,7 @@
     grad_query, grad_key, grad_value, log_total, delta_all, grad_bias = lax.cond(
         own_tile > 0.5, run_queries, skip_queries
     )
-    bias_summed = lax.psum(grad_bias, ("row", "col"))
+    bias_summed = jnp.sum(lax.all_gather(grad_bias, ("row", "col")), axis=0)
     query_grads = grad_query.astype(jnp.bfloat16).reshape(tile_rows, tile_cols, model_width)
     partials = jnp.stack((grad_key, grad_value)).reshape(2, padded_rows, padded_cols, model_width)
     owned_grads = fold_rows(fold_columns(partials, radius), radius)

time: 249 us -> 259 us (1.040)
  blocking collectives: 50.8 us -> 59 us
    all_gather x0 -> x1, blocking collectives: none -> 59 us  [shards(): bias_summed = jnp.sum(lax.all_gather(grad_bias, ('row', 'col')), axis=0)]
    psum x1 -> x0, blocking collectives: 50.8 us -> none  [shards(): bias_summed = lax.psum(grad_bias, ('row', 'col'))]
where the time goes in v1:
time: 259 us; the launch traced here: 256 us
  starting transfers between devices  173 us (67%)
  blocking collectives  59 us (23%)
  waiting for transfers between devices  9.37 us (4%)
  local copies, waits for them, and re-layouts  8.09 us (3%)
  other arithmetic  4.62 us (2%)
    ppermute x4, starting transfers between devices, from_behind(): lax.ppermute(value, axis, [(source, source + steps) for source in range(f...  164 us
    all_gather x1, blocking collectives, shards(): bias_summed = jnp.sum(lax.all_gather(grad_bias, ('row', 'col')), axis=0)  59 us
    ppermute x2, waiting for transfers between devices, with_halo(): lax.ppermute(lax.slice_in_dim(block, 0, width, axis=dim), axis, backward)  7.05 us
    ppermute x2, starting transfers between devices, with_halo(): lax.ppermute(lax.slice_in_dim(block, block.shape[dim] - width, None, axis...  6.83 us
  transfers between devices with their start and end apart: 8, of which 4 were waited for; matrix products, arithmetic and copies ran while one was open for 1% of the time, Pallas kernels for 0%

profile of v1, /device:TPU:0, one launch (start us, length us, event | category | flops | bytes accessed | tf_op | source)
XLA Modules:
  0.0 256.0 jit_solution(1405224396193310682)
XLA Ops:
  0.6 1.0 pad_maximum_fusion.2
  1.6 1.3 collective-permute-start.1
  2.9 5.5 %collective-permute-start = (bf16[2,8,16,512]{3,2,1,0:T(8,128)(2,1)S(1)}, bf16[2,8,16,512]{3,2,1,0:T(8,128)(2,1)S(1)}, u32[]{:S(2)}, u32[]{:S(2)}) collective-permute-start(bf16[2,8,16,512]{3,2,1,0:T(8,128)(2,1)S(1)} %pad_maximum_fusion.2), channel_id=1, source_target_pairs={{0,8},{8,16},{16,24},{1,9},{9,17},{17,25},{2,10},{10,18},{18,26},{... | collective-permute-start | bytes 786440 | tf_op jit(solution)/shard_map/ppermute | solution.py:18
  8.5 0.8 fusion.52
  9.3 0.2 fusion.49
  9.4 0.0 copy-start.3
  9.4 0.0 copy-start.4
  9.4 4.2 %collective-permute-done.1 = bf16[2,8,16,512]{3,2,1,0:T(8,128)(2,1)S(1)} collective-permute-done((bf16[2,8,16,512]{3,2,1,0:T(8,128)(2,1)S(1)}, bf16[2,8,16,512]{3,2,1,0:T(8,128)(2,1)S(1)}, u32[]{:S(2)}, u32[]{:S(2)}) %collective-permute-start.1) | collective-permute-done | bytes 262176 | tf_op jit(solution)/shard_map/ppermute | solution.py:21
  13.7 0.3 collective-permute-done
  14.0 1.1 pad_maximum_fusion.1
  15.0 0.1 fusion.59
  15.1 1.3 collective-permute-start.2
  16.4 1.3 collective-permute-start.3
  17.7 0.6 slice.176
  19.0 0.2 fusion.48
  19.2 0.0 collective-permute-done.2
  19.2 2.8 %collective-permute-done.3 = bf16[2,24,8,512]{3,2,1,0:T(8,128)(2,1)S(1)} collective-permute-done((bf16[2,24,8,512]{3,2,1,0:T(8,128)(2,1)S(1)}, bf16[2,24,8,512]{3,2,1,0:T(8,128)(2,1)S(1)}, u32[]{:S(2)}, u32[]{:S(2)}) %collective-permute-start.3) | collective-permute-done | bytes 393248 | tf_op jit(solution)/shard_map/ppermute | solution.py:21
  22.1 0.0 copy-done.3
  22.1 0.0 copy-done.4
  22.1 0.2 pad_maximum_fusion
  22.3 3.4 %conditional.1 = (f32[8,17,17]{2,1,0:T(8,128)S(1)}, bf16[8,16,512]{2,1,0:T(8,128)(2,1)}, f32[1,24,32,512]{3,2,1,0:T(8,128)}, f32[1,24,32,512]{3,2,1,0:T(8,128)}) conditional(s32[]{:T(128)} %bitcast.7, () %tuple.69, (bf16[8,16,512]{2,1,0:T(8,128)(2,1)}, bf16[2,24,32,512]{3,2,1,0:T(8,128)(2,1)S(1)}, bf16[8,16,512]{2,1,0:T(8,128)(2,1)}, ...), branch_computations={%region_0.1_spmd, %region_1.11_spmd} | conditional | flops 72604152 | bytes 37085184 | solution.py:220
  22.3 0.7 reshape.255
  23.0 1.4 stack.5.clone
  24.3 1.3 stack.5
  25.7 1.5 constant_dynamic-update-slice_fusion.1
  27.2 1.5 constant_dynamic-update-slice_fusion
  28.7 0.2 convert.13
  29.0 0.1 fusion.57
  29.1 155.1 %collective-permute-start.4 = (bf16[2,24,8,512]{3,2,1,0:T(8,128)(2,1)S(1)}, bf16[2,24,8,512]{3,2,1,0:T(8,128)(2,1)S(1)}, u32[]{:S(2)}, u32[]{:S(2)}) collective-permute-start(bf16[2,24,8,512]{3,2,1,0:T(8,128)(2,1)S(1)} %get-tuple-element.631), channel_id=1, source_target_pairs={{0,1},{1,2},{2,3},{3,4},{4,5},{5,6},{6,7},{8,9},{9,10},{10,11},{11... | collective-permute-start | bytes 1179656 | tf_op jit(solution)/shard_map/ppermute | solution.py:10
  184.1 1.3 collective-permute-start.5
  185.4 0.2 slice.195
  185.6 0.0 collective-permute-done.4
  185.6 0.1 fusion.43
  185.8 2.0 collective-permute-done.5
  187.8 0.2 fusion.42
  188.0 0.1 convert.14
  188.1 5.9 %collective-permute-start.6 = (bf16[2,8,16,512]{3,2,1,0:T(8,128)(2,1)S(1)}, bf16[2,8,16,512]{3,2,1,0:T(8,128)(2,1)S(1)}, u32[]{:S(2)}, u32[]{:S(2)}) collective-permute-start(bf16[2,8,16,512]{3,2,1,0:T(8,128)(2,1)S(1)} %get-tuple-element.632), channel_id=1, source_target_pairs={{0,8},{8,16},{16,24},{1,9},{9,17},{17,25},{2,10},{10,18},{18,26},{... | collective-permute-start | bytes 786440 | tf_op jit(solution)/shard_map/ppermute | solution.py:10
  194.1 1.3 collective-permute-start.7
  195.4 59.0 %all-gather = f32[256,17,17]{2,0,1:T(8,128)S(1)} all-gather(f32[8,17,17]{2,0,1:T(8,128)S(1)} %copy.61), channel_id=2, replica_groups=mesh['row'=4,'col'=8] {'row','col'}, dimensions={0}, use_global_device_ids=true | all-gather | bytes 305184 | tf_op jit(solution)/shard_map/all_gather | solution.py:223
  254.4 0.8 bitcast_reduce_fusion
  255.2 0.0 collective-permute-done.6
  255.2 0.0 collective-permute-done.7
  255.2 0.1 fusion.45
  255.3 0.7 slice_bitcast_fusion
  (7 shorter events, 0.1 us)
Async XLA Ops:
  1.6 12.0 %collective-permute-start.1 = (bf16[2,8,16,512]{3,2,1,0:T(8,128)(2,1)S(1)}, bf16[2,8,16,512]{3,2,1,0:T(8,128)(2,1)S(1)}, u32[]{:S(2)}, u32[]{:S(2)}) collective-permute-start(bf16[2,8,16,512]{3,2,1,0:T(8,128)(2,1)S(1)} %pad_maximum_fusion.2), channel_id=1, source_target_pairs={{8,0},{16,8},{24,16},{9,1},{17,9},{25,17},{10,2},{18,10},{26,18},{... | collective-permute-start | bytes 786440 | tf_op jit(solution)/shard_map/ppermute | solution.py:21
  2.9 11.1 %collective-permute-start = (bf16[2,8,16,512]{3,2,1,0:T(8,128)(2,1)S(1)}, bf16[2,8,16,512]{3,2,1,0:T(8,128)(2,1)S(1)}, u32[]{:S(2)}, u32[]{:S(2)}) collective-permute-start(bf16[2,8,16,512]{3,2,1,0:T(8,128)(2,1)S(1)} %pad_maximum_fusion.2), channel_id=1, source_target_pairs={{0,8},{8,16},{16,24},{1,9},{9,17},{17,25},{2,10},{10,18},{18,26},{... | collective-permute-start | bytes 786440 | tf_op jit(solution)/shard_map/ppermute | solution.py:18
  9.4 12.6 %copy-start.3 = (bf16[8,16,512]{2,1,0:T(8,128)(2,1)S(1)}, bf16[8,16,512]{2,1,0:T(8,128)(2,1)}, u32[]{:S(2)}) copy-start(bf16[8,16,512]{2,1,0:T(8,128)(2,1)} %param.24) | copy-start | bytes 393220
  9.4 12.6 %copy-start.4 = (bf16[8,16,512]{2,1,0:T(8,128)(2,1)S(1)}, bf16[8,16,512]{2,1,0:T(8,128)(2,1)}, u32[]{:S(2)}) copy-start(bf16[8,16,512]{2,1,0:T(8,128)(2,1)} %param.23) | copy-start | bytes 393220
  15.1 4.1 %collective-permute-start.2 = (bf16[2,24,8,512]{3,2,1,0:T(8,128)(2,1)S(1)}, bf16[2,24,8,512]{3,2,1,0:T(8,128)(2,1)S(1)}, u32[]{:S(2)}, u32[]{:S(2)}) collective-permute-start(bf16[2,24,8,512]{3,2,1,0:T(8,128)(2,1)S(1)} %get-tuple-element.634), channel_id=1, source_target_pairs={{0,1},{1,2},{2,3},{3,4},{4,5},{5,6},{6,7},{8,9},{9,10},{10,11},{11... | collective-permute-start | bytes 1179656 | tf_op jit(solution)/shard_map/ppermute | solution.py:18
  16.4 5.6 %collective-permute-start.3 = (bf16[2,24,8,512]{3,2,1,0:T(8,128)(2,1)S(1)}, bf16[2,24,8,512]{3,2,1,0:T(8,128)(2,1)S(1)}, u32[]{:S(2)}, u32[]{:S(2)}) collective-permute-start(bf16[2,24,8,512]{3,2,1,0:T(8,128)(2,1)S(1)} %get-tuple-element.635), channel_id=1, source_target_pairs={{1,0},{2,1},{3,2},{4,3},{5,4},{6,5},{7,6},{9,8},{10,9},{11,10},{12... | collective-permute-start | bytes 1179656 | tf_op jit(solution)/shard_map/ppermute | solution.py:21
  29.1 156.6 %collective-permute-start.4 = (bf16[2,24,8,512]{3,2,1,0:T(8,128)(2,1)S(1)}, bf16[2,24,8,512]{3,2,1,0:T(8,128)(2,1)S(1)}, u32[]{:S(2)}, u32[]{:S(2)}) collective-permute-start(bf16[2,24,8,512]{3,2,1,0:T(8,128)(2,1)S(1)} %get-tuple-element.631), channel_id=1, source_target_pairs={{0,1},{1,2},{2,3},{3,4},{4,5},{5,6},{6,7},{8,9},{9,10},{10,11},{11... | collective-permute-start | bytes 1179656 | tf_op jit(solution)/shard_map/ppermute | solution.py:10
  184.1 3.6 %collective-permute-start.5 = (bf16[2,24,8,512]{3,2,1,0:T(8,128)(2,1)S(1)}, bf16[2,24,8,512]{3,2,1,0:T(8,128)(2,1)S(1)}, u32[]{:S(2)}, u32[]{:S(2)}) collective-permute-start(bf16[2,24,8,512]{3,2,1,0:T(8,128)(2,1)S(1)} %get-tuple-element.630), channel_id=1, source_target_pairs={{1,0},{2,1},{3,2},{4,3},{5,4},{6,5},{7,6},{9,8},{10,9},{11,10},{12... | collective-permute-start | bytes 1179656 | tf_op jit(solution)/shard_map/ppermute | solution.py:10
  188.1 67.0 %collective-permute-start.6 = (bf16[2,8,16,512]{3,2,1,0:T(8,128)(2,1)S(1)}, bf16[2,8,16,512]{3,2,1,0:T(8,128)(2,1)S(1)}, u32[]{:S(2)}, u32[]{:S(2)}) collective-permute-start(bf16[2,8,16,512]{3,2,1,0:T(8,128)(2,1)S(1)} %get-tuple-element.632), channel_id=1, source_target_pairs={{0,8},{8,16},{16,24},{1,9},{9,17},{17,25},{2,10},{10,18},{18,26},{... | collective-permute-start | bytes 786440 | tf_op jit(solution)/shard_map/ppermute | solution.py:10
  194.1 61.1 %collective-permute-start.7 = (bf16[2,8,16,512]{3,2,1,0:T(8,128)(2,1)S(1)}, bf16[2,8,16,512]{3,2,1,0:T(8,128)(2,1)S(1)}, u32[]{:S(2)}, u32[]{:S(2)}) collective-permute-start(bf16[2,8,16,512]{3,2,1,0:T(8,128)(2,1)S(1)} %get-tuple-element.633), channel_id=1, source_target_pairs={{8,0},{16,8},{24,16},{9,1},{17,9},{25,17},{10,2},{18,10},{26,18},{... | collective-permute-start | bytes 786440 | tf_op jit(solution)/shard_map/ppermute | solution.py:10
